TPU v7x, 32 devices: a whole 2x2x4 slice. The times are simulated.
32 devices in a mesh: row: 4 (over z), col: 8 (over y, x, core).
Axes of the slice: x: 2, y: 2, z: 4, core: 2. Of those that a mesh axis runs over, the one named last changes fastest.
Arguments:
- activations: bfloat16 [4096, 8192], P('row', 'col'), may hold values from -6 to 6
- errors: bfloat16 [4096, 8192], P('row', 'col'), may hold values from -6 to 6
- act_proj: bfloat16 [8192, 128], P('col'), may hold values from -0.0625 to 0.0625
- err_proj: bfloat16 [8192, 128], P('col'), may hold values from -0.0625 to 0.0625
- lengths: int32 [4, 64], P('row'), may hold values from 1 to 256, 1024 in all within a row
- ridge: float32 [16384, 16384], P('row', 'col'), may hold values from -4 to 36, as said below
- pivot_inverse: float32 [2, 512, 512], replicated, may hold values from -1 to 1
Outputs:
- eliminated: float32 [16384, 16384], P('row', 'col')
Inputs may be any that keep to these rules, and one draw needn't show every extreme that they name: The lengths of one row group sum to 1024. `ridge`: Symmetric.
All inputs are finite; a program needn't handle non-finite values.
Results may differ from a plain program's by a relative error of at most 0.0074.
Values may be sent and summed in bfloat16 or wider, within the bound.
No kernel may reach another device: no remote copies, remote signals or barrier semaphores. Data moves between devices by JAX's collectives and lax.ppermute only.
A program may use at most 192 MiB of HBM per device.

v0:
```python
import jax
import jax.numpy as jnp
from jax import lax
from jax.sharding import PartitionSpec as P


def spread_2(array, axis, root):
    mine = lax.axis_index(axis) == root
    return lax.psum(jnp.where(mine, array, jnp.zeros_like(array)), axis)


def as_sent(array):

    def short(part):
        return part.astype(jnp.bfloat16) if part.dtype == jnp.float32 else part

    return jax.tree.map(short, array)


def per_device(activations, errors, act_proj, err_proj, lengths, ridge, pivot_inverse):
    part_act = jnp.dot(activations, act_proj, preferred_element_type=jnp.float32)
    part_err = jnp.dot(errors, err_proj, preferred_element_type=jnp.float32)
    summed_act, summed_err = lax.psum((part_act, part_err), "col")
    proj_act = summed_act.astype(jnp.bfloat16)
    col_count = lax.axis_size("col")
    row_count = lax.axis_size("row")
    col_ratio = col_count // row_count
    col_idx = lax.axis_index("col")
    row_idx = lax.axis_index("row")
    proj_width = act_proj.shape[1]
    err_share = proj_width // col_count
    err_part = lax.dynamic_slice_in_dim(summed_err, col_idx * err_share, err_share, 1).astype(
        jnp.bfloat16
    )
    lengths_row = lengths[0]
    captions_dev = lengths_row.shape[0]
    tokens_dev = activations.shape[0]
    caption_end = jnp.cumsum(lengths_row)
    caption_start = caption_end - lengths_row
    positions = jnp.arange(tokens_dev, dtype=jnp.int32)[:, None]
    member = ((positions >= caption_start[None, :]) & (positions < caption_end[None, :])).astype(
        jnp.bfloat16
    )
    weighted = (member[:, :, None] * err_part[:, None, :]).reshape(
        tokens_dev, captions_dev * err_share
    )
    local_grads = lax.dot_general(
        weighted, proj_act, (((0,), (0,)), ((), ())), preferred_element_type=jnp.float32
    )
    local_grads = local_grads.reshape(captions_dev, err_share * proj_width).astype(jnp.bfloat16)
    col_grads = lax.all_gather(local_grads, "row", axis=0, tiled=True)
    row_parts = []
    for column_step in range(col_ratio):
        row_parts.append(spread_2(col_grads, "col", row_idx * col_ratio + column_step))
    row_grads = jnp.concatenate(row_parts, axis=1)
    captions_all = col_grads.shape[0]
    gram_tile = lax.dot_general(
        row_grads, col_grads, (((0,), (0,)), ((), ())), preferred_element_type=jnp.float32
    )
    matrix = ridge + gram_tile / captions_all
    tile_rows, tile_cols = ridge.shape
    row_start = row_idx * tile_rows
    col_start = col_idx * tile_cols
    row_ids = row_start + jnp.arange(tile_rows, dtype=jnp.int32)
    col_ids = col_start + jnp.arange(tile_cols, dtype=jnp.int32)
    panel_width = pivot_inverse.shape[1]

    def apply_inverse(columns, start_col, inverse):
        result = jnp.dot(columns, inverse.T, precision=lax.Precision.HIGHEST)
        return jnp.where(row_ids[:, None] >= start_col, result, 0.0)

    first_panel = apply_inverse(matrix[:, 0:panel_width], 0, pivot_inverse[0])
    pivot_block = spread_2(
        first_panel[panel_width : 2 * panel_width].astype(jnp.bfloat16), "row", 0
    ).astype(jnp.float32)
    lower_first = jnp.where(row_ids[:, None] >= panel_width, first_panel, 0.0)
    second_block = matrix[:, panel_width : 2 * panel_width] - jnp.dot(
        lower_first, pivot_block.T, precision=lax.Precision.HIGHEST
    )
    second_panel = apply_inverse(second_block, panel_width, pivot_inverse[1])
    both_panels = jnp.concatenate([first_panel, second_panel], axis=1)
    row_panel = spread_2(as_sent(both_panels), "col", 0).astype(both_panels.dtype)
    col_piece = lax.dynamic_slice_in_dim(row_panel, col_idx % col_ratio * tile_cols, tile_cols, 0)
    col_panel = spread_2(as_sent(col_piece), "row", col_idx // col_ratio).astype(col_piece.dtype)
    row_panel, col_panel = (row_panel, col_panel)
    current = matrix
    stop_col = 2 * panel_width
    lower_part = jnp.where(row_ids[:, None] >= stop_col, row_panel, 0.0)
    upper_part = jnp.where(col_ids[:, None] >= stop_col, col_panel, 0.0)
    current = current - jnp.dot(lower_part, upper_part.T, precision=lax.Precision.HIGHEST)
    offset = jnp.clip(0 - col_start, 0, tile_cols - (stop_col - 0))
    placed = lax.dynamic_update_slice(jnp.zeros_like(current), row_panel, (jnp.int32(0), offset))
    in_panel = (col_ids >= 0) & (col_ids < stop_col)
    current = jnp.where(in_panel[None, :], placed, current)
    above_panel = ((row_ids >= 0) & (row_ids < stop_col))[:, None] & (col_ids >= stop_col)[None, :]
    return jnp.where(above_panel, 0.0, current)


def solution(mesh):
    in_specs = (
        P("row", "col"),
        P("row", "col"),
        P("col", None),
        P("col", None),
        P("row", None),
        P("row", "col"),
        P(),
    )
    out_specs = P("row", "col")
    return jax.shard_map(
        per_device, mesh=mesh, in_specs=in_specs, out_specs=out_specs, check_vma=False
    )
```

profile of v0, /device:TPU:0, one launch (start us, length us, event | category | flops | bytes accessed | tf_op | source)
XLA Modules:
  0.0 710.1 jit_solution(3458219125566349725)
XLA Ops:
  6.5 1.6 copy-done
  8.1 1.8 fusion.41
  9.9 2.3 fusion.42
  12.2 0.7 copy.12
  13.0 0.1 reduce
  13.2 0.7 fusion.37
  13.8 0.1 fusion.27
  13.9 52.8 %all-reduce.15 = (bf16[1024,128]{0,1:T(8,128)(2,1)S(1)}, bf16[1024,128]{1,0:T(8,128)(2,1)S(1)}) all-reduce(f32[1024,128]{0,1:T(8,128)S(1)} %fusion.41, f32[1024,128]{1,0:T(8,128)S(1)} %fusion.42), channel_id=1, replica_groups=mesh['row'=4,'col'=8] {'col'}, use_global_device_ids=true, to_apply=%region_1.0 | all-reduce | flops 262144 | bytes 1572864 | tf_op jit(solution)/shard_map/psum | solution.py:23
  66.8 0.2 broadcast_multiply_fusion
  67.0 0.7 convolution_convert_fusion
  67.7 0.8 convert_element_type.35
  68.6 27.7 %all-gather.2.cloned.1.call-done = bf16[256,2048]{1,0:T(8,128)(2,1)} async-done(((bf16[64,2048]{1,0:T(8,128)(2,1)}), bf16[256,2048]{1,0:T(8,128)(2,1)}) %all-gather.2.cloned.1.call-update) | async-done | bytes 1048592 | tf_op jit(solution)/shard_map/all_gather | solution.py:51
  96.3 2.7 broadcast_select_fusion.1
  99.0 61.7 %all-reduce.14.cloned.1.call-done = (bf16[256,2048]{1,0:T(8,128)(2,1)}, bf16[256,2048]{1,0:T(8,128)(2,1)}) async-done(((bf16[256,2048]{1,0:T(8,128)(2,1)}, bf16[256,2048]{1,0:T(8,128)(2,1)}), (bf16[256,2048]{1,0:T(8,128)(2,1)}, bf16[256,2048]{1,0:T(8,128)(2,1)})) %all-reduce.14.cloned.1.call-update) | async-done | bytes 2097168 | tf_op jit(solution)/shard_map/psum | solution.py:9
  160.8 25.6 %multiply_add_fusion = f32[4096,2048]{1,0:T(8,128)} fusion(f32[4096,2048]{1,0:T(8,128)} %param.12, bf16[256,2048]{1,0:T(8,128)(2,1)} %all-gather.2.cloned.1.call-done, bf16[256,2048]{1,0:T(8,128)(2,1)} %get-tuple-element.7, bf16[256,2048]{1,0:T(8,128)(2,1)} %get-tuple-element.8), kind=kOutput, calls=%fused_computation.1 | convolution fusion | flops 4315938816 | bytes 70254592 | tf_op jit(solution)/shard_map/dot_general | solution.py:57
  186.4 18.0 %select_convert_fusion.1 = (bf16[4096,512]{1,0:T(8,128)(2,1)S(1)}, f32[4096,512]{1,0:T(8,128)}) fusion(pred[4096]{0:T(1024)(128)(4,1)S(1)} %fusion.31, f32[2,512,512]{2,1,0:T(8,128)S(1)} %copy-done.4, f32[4096,2048]{1,0:T(8,128)} %multiply_add_fusion), kind=kOutput, calls=%fused_computation.17 | convolution fusion | flops 12886999040 | bytes 22024192 | tf_op jit(solution)/shard_map/dot_general | solution.py:69
  204.4 2.0 copy-done.2
  206.5 0.9 slice_select_fusion
  207.4 0.2 all-reduce.10.cloned.1.call-start
  207.6 37.6 %all-reduce.8.cloned.1.call-done = bf16[512,512]{1,0:T(8,128)(2,1)} async-done(((bf16[512,512]{1,0:T(8,128)(2,1)}), bf16[512,512]{1,0:T(8,128)(2,1)}) %all-reduce.8.cloned.1.call-update) | async-done | bytes 524304 | tf_op jit(solution)/shard_map/psum | solution.py:9
  245.2 9.5 %fusion.7 = f32[4096,512]{1,0:T(8,128)S(1)} fusion(bf16[512,512]{1,0:T(8,128)(2,1)} %all-reduce.8.cloned.1.call-done, f32[4096,512]{1,0:T(8,128)} %get-tuple-element.12, pred[4096]{0:T(1024)(128)(4,1)S(1)} %fusion.29, pred[4096]{0:T(1024)(128)(4,1)S(1)} %fusion.31), kind=kOutput, calls=%fused_computation.13 | convolution fusion | flops 12889096192 | bytes 17309696 | tf_op jit(solution)/shard_map/dot_general | solution.py:77
  254.7 16.7 %select_convert_fusion = bf16[4096,512]{1,0:T(8,128)(2,1)S(1)} fusion(f32[4096,512]{1,0:T(8,128)S(1)} %fusion.7, f32[4096,2048]{1,0:T(8,128)} %multiply_add_fusion, pred[4096]{0:T(1024)(128)(4,1)S(1)} %fusion.29, f32[2,512,512]{2,1,0:T(8,128)S(1)} %copy-done.4), kind=kOutput, calls=%fused_computation.12 | convolution fusion | flops 12891193344 | bytes 22024192 | tf_op jit(solution)/shard_map/dot_general | solution.py:69
  271.4 4.3 maximum_select_fusion
  275.8 0.3 all-reduce.12.cloned.1.call-start
  276.1 125.9 %all-reduce.10.cloned.1.call-done = bf16[4096,1024]{1,0:T(8,128)(2,1)} async-done(((bf16[4096,1024]{1,0:T(8,128)(2,1)}), bf16[4096,1024]{1,0:T(8,128)(2,1)}) %all-reduce.10.cloned.1.call-update) | async-done | bytes 8388624 | tf_op jit(solution)/shard_map/psum | solution.py:9
  401.9 11.2 %convert_element_type.36 = f32[4096,1024]{1,0:T(8,128)} convert(bf16[4096,1024]{1,0:T(8,128)(2,1)} %all-reduce.10.cloned.1.call-done) | non-fusion elementwise | flops 4194304 | bytes 25165824 | tf_op jit(solution)/shard_map/convert_element_type | solution.py:82
  413.2 6.6 fusion.11
  419.8 11.5 %broadcast_in_dim.81 = f32[4096,2048]{1,0:T(8,128)} broadcast(f32[]{:T(128)} %constant.29.clone.1), dimensions={} | broadcast | bytes 33554436 | tf_op jit(solution)/shard_map/jit(_where)/broadcast_in_dim | solution.py:96
  431.4 78.0 %dynamic_update_slice.3 = f32[4096,2048]{1,0:T(8,128)} dynamic-update-slice(f32[4096,2048]{1,0:T(8,128)} %broadcast_in_dim.81, f32[4096,1024]{1,0:T(8,128)} %convert_element_type.36, s32[]{:T(128)} %constant.24.clone.1, s32[]{:T(128)S(6)} %min.4) | dynamic-update-slice | bytes 33554436 | tf_op jit(solution)/shard_map/dynamic_update_slice | solution.py:92
  509.4 65.7 %all-reduce.12.cloned.1.call-done = bf16[2048,1024]{1,0:T(8,128)(2,1)} async-done(((bf16[2048,1024]{1,0:T(8,128)(2,1)}), bf16[2048,1024]{1,0:T(8,128)(2,1)}) %all-reduce.12.cloned.1.call-update) | async-done | bytes 4194320 | tf_op jit(solution)/shard_map/psum | solution.py:9
  575.0 5.2 fusion.57
  580.2 123.4 %select_select_fusion = f32[4096,2048]{1,0:T(8,128)} fusion(f32[4096,2048]{1,0:T(8,128)} %dynamic_update_slice.3, f32[4096,2048]{1,0:T(8,128)} %multiply_add_fusion, pred[2048]{0:T(1024)(128)(4,1)S(1)} %get-tuple-element.16, pred[2048]{0:T(1024)(128)(4,1)S(1)} %get-tuple-element.15, pred[4096]{0:T(1024)(128)(4,1)S(1)} %get-tuple-element.14, ...), kind=kOutput, calls=%fused_computation | convolution fusion | flops 103121158144 | bytes 117452800 | tf_op jit(solution)/shard_map/dot_general | solution.py:90
  (22 shorter events, 0.3 us)
Async XLA Ops:
  6.5 1.6 copy-start
  6.5 89.7 %all-gather.2.cloned.1.call-start = ((), (), s32[]{:S(2)}) async-start(), calls=%async_computation | async-start | bytes 1310720 | tf_op jit(solution)/shard_map/all_gather | solution.py:51
  68.5 92.2 %all-reduce.14.cloned.1.call-start = ((), (), s32[]{:S(2)}) async-start(), calls=%async_computation.4 | async-start | bytes 4194304 | tf_op jit(solution)/shard_map/psum | solution.py:9
  99.0 146.3 %all-reduce.8.cloned.1.call-start = ((), (), s32[]{:S(2)}) async-start(), calls=%async_computation.1 | async-start | bytes 1048576 | tf_op jit(solution)/shard_map/psum | solution.py:9
  160.8 25.6 %copy-start.4 = (f32[2,512,512]{2,1,0:T(8,128)S(1)}, f32[2,512,512]{2,1,0:T(8,128)}, u32[]{:S(2)}) copy-start(f32[2,512,512]{2,1,0:T(8,128)} %param.13) | copy-start | bytes 6291460
  204.4 2.0 copy-start.2
  207.4 194.6 %all-reduce.10.cloned.1.call-start = ((), (), s32[]{:S(2)}) async-start(), calls=%async_computation.2 | async-start | bytes 16777216 | tf_op jit(solution)/shard_map/psum | solution.py:9
  254.7 16.7 %copy-start.3 = (bf16[4096,512]{1,0:T(8,128)(2,1)S(1)}, bf16[4096,512]{1,0:T(8,128)(2,1)}, u32[]{:S(2)}) copy-start(bf16[4096,512]{1,0:T(8,128)(2,1)} %copy-done.2) | copy-start | bytes 12582916
  275.8 299.3 %all-reduce.12.cloned.1.call-start = ((), (), s32[]{:S(2)}) async-start(), calls=%async_computation.3 | async-start | bytes 8388608 | tf_op jit(solution)/shard_map/psum | solution.py:9
  580.2 123.4 %copy-start.1 = (bf16[1024,1024]{1,0:T(8,128)(2,1)S(1)}, bf16[1024,1024]{1,0:T(8,128)(2,1)}, u32[]{:S(2)}) copy-start(bf16[1024,1024]{1,0:T(8,128)(2,1)} %param.8) | copy-start | bytes 6291460
Sparse Core Ops, SparseCore 0:
  68.7 27.5 all-gather.1
  99.5 61.1 all-reduce.13
  207.5 37.6 all-reduce.7
  275.9 125.9 all-reduce.9
  419.9 155.1 all-reduce.11
where the time goes:
time: 712 us; the launch traced here: 710 us
  waiting for transfers between devices  319 us (45%)
  matrix products  198 us (28%)
  local copies, waits for them, and re-layouts  94.8 us (13%)
  blocking collectives  52.8 us (7%)
  other arithmetic  32 us (4%)
  between operations  13.3 us (2%)
    psum x4, waiting for transfers between devices, spread_2(): return lax.psum(jnp.where(mine, array, jnp.zeros_like(array)), axis)  291 us
    dot_general x1, matrix products, per_device(): jnp.dot(lower_part, upper_part.T, precision=lax.Precision.HIGHEST)  123 us
    dynamic_update_slice x1, local copies, waits for them, and re-layouts, per_device(): lax.dynamic_update_slice(jnp.zeros_like(current), row_panel, (jnp.int32(0...  78 us
    psum x1, blocking collectives, per_device(): summed_act, summed_err = lax.psum((part_act, part_err), 'col')  52.8 us
    dot_general x2, matrix products, apply_inverse(): result = jnp.dot(columns, inverse.T, precision=lax.Precision.HIGHEST)  34.7 us
    all_gather x1, waiting for transfers between devices, per_device(): col_grads = lax.all_gather(local_grads, 'row', axis=0, tiled=True)  27.7 us
    dot_general x1, matrix products, per_device(): lax.dot_general(row_grads, col_grads, (((0,), (0,)), ((), ())), preferred...  25.6 us
    select_n x4, other arithmetic, spread_2(): return lax.psum(jnp.where(mine, array, jnp.zeros_like(array)), axis)  14.4 us
  transfers between devices with their start and end apart: 5, of which 5 were waited for; matrix products, arithmetic and copies ran while one was open for 13% of the time, Pallas kernels for 0%

commit v1 on v0

--- a/solution.py
+++ b/solution.py
@@ -6,7 +6,7 @@
 
 def spread_2(array, axis, root):
     mine = lax.axis_index(axis) == root
-    return lax.psum(jnp.where(mine, array, jnp.zeros_like(array)), axis)
+    return jnp.sum(lax.all_gather(jnp.where(mine, array, jnp.zeros_like(array)), axis), axis=0)
 
 
 def as_sent(array):

time: 712 us -> 1140 us (1.60)
  waiting for transfers between devices: 319 us -> 674 us
  other arithmetic: 32 us -> 84 us
  local copies, waits for them, and re-layouts: 94.8 us -> 112 us
    all_gather x0 -> x5, waiting for transfers between devices: none -> 646 us  [spread_2(): lax.all_gather(jnp.where(mine, array, jnp.zeros_like(array)), axis)]
    psum x4 -> x0, waiting for transfers between devices: 291 us -> none  [spread_2(): return lax.psum(jnp.where(mine, array, jnp.zeros_like(array)), axis)]
    reduce_sum x0 -> x5, other arithmetic: none -> 51.5 us  [spread_2(): jnp.sum(lax.all_gather(jnp.where(mine, array, jnp.zeros_like(array)), axi...]
    select_n x0 -> x1, local copies, waits for them, and re-layouts: none -> 12 us  [spread_2(): jnp.where(mine, array, jnp.zeros_like(array))]
  transfers between devices with their start and end apart: 5 -> 6, of which waited for: 5 -> 6; matrix products, arithmetic and copies ran while one was open for 13% -> 9% of each run, Pallas kernels for 0% -> 0%
where the time goes in v1:
time: 1140 us; the launch traced here: 1130 us
  waiting for transfers between devices  674 us (59%)
  matrix products  197 us (17%)
  local copies, waits for them, and re-layouts  112 us (10%)
  other arithmetic  84 us (7%)
  blocking collectives  52.8 us (5%)
  between operations  13.9 us (1%)
    all_gather x5, waiting for transfers between devices, spread_2(): lax.all_gather(jnp.where(mine, array, jnp.zeros_like(array)), axis)  646 us
    dot_general x1, matrix products, per_device(): jnp.dot(lower_part, upper_part.T, precision=lax.Precision.HIGHEST)  124 us
    dynamic_update_slice x1, local copies, waits for them, and re-layouts, per_device(): lax.dynamic_update_slice(jnp.zeros_like(current), row_panel, (jnp.int32(0...  78.1 us
    psum x1, blocking collectives, per_device(): summed_act, summed_err = lax.psum((part_act, part_err), 'col')  52.8 us
    reduce_sum x5, other arithmetic, spread_2(): jnp.sum(lax.all_gather(jnp.where(mine, array, jnp.zeros_like(array)), axi...  51.5 us
    dot_general x2, matrix products, apply_inverse(): result = jnp.dot(columns, inverse.T, precision=lax.Precision.HIGHEST)  34 us
    all_gather x1, waiting for transfers between devices, per_device(): col_grads = lax.all_gather(local_grads, 'row', axis=0, tiled=True)  27.7 us
    dot_general x1, matrix products, per_device(): lax.dot_general(row_grads, col_grads, (((0,), (0,)), ((), ())), preferred...  24.9 us
  transfers between devices with their start and end apart: 6, of which 6 were waited for; matrix products, arithmetic and copies ran while one was open for 9% of the time, Pallas kernels for 0%

profile of v1, /device:TPU:0, one launch (start us, length us, event | category | flops | bytes accessed | tf_op | source)
XLA Modules:
  0.0 1134.5 jit_solution(2922848804791710989)
XLA Ops:
  6.5 1.6 copy-done
  8.1 1.8 fusion.42
  9.9 2.3 fusion.43
  13.9 52.8 %all-reduce.2 = (bf16[1024,128]{0,1:T(8,128)(2,1)S(1)}, bf16[1024,128]{1,0:T(8,128)(2,1)S(1)}) all-reduce(f32[1024,128]{0,1:T(8,128)S(1)} %fusion.42, f32[1024,128]{1,0:T(8,128)S(1)} %fusion.43), channel_id=1, replica_groups=mesh['row'=4,'col'=8] {'col'}, use_global_device_ids=true, to_apply=%region_1.0 | all-reduce | flops 262144 | bytes 1572864 | tf_op jit(solution)/shard_map/psum | solution.py:23
  67.7 0.8 convert_element_type.52
  68.6 27.7 %all-gather.11.cloned.1.call-done = bf16[256,2048]{1,0:T(8,128)(2,1)} async-done(((bf16[64,2048]{1,0:T(8,128)(2,1)}), bf16[256,2048]{1,0:T(8,128)(2,1)}) %all-gather.11.cloned.1.call-update) | async-done | bytes 1048592 | tf_op jit(solution)/shard_map/all_gather | solution.py:51
  96.3 2.7 broadcast_select_fusion.1
  100.1 52.7 %all-gather.15.cloned.1.call-done = bf16[2048,2048]{1,0:T(8,128)(2,1)} async-done(((bf16[256,2048]{1,0:T(8,128)(2,1)}), bf16[2048,2048]{1,0:T(8,128)(2,1)}) %all-gather.15.cloned.1.call-update) | async-done | bytes 8388624 | tf_op jit(solution)/shard_map/all_gather | solution.py:9
  152.8 5.3 reduce_sum.60
  158.1 50.9 %all-gather.17.cloned.1.call-done = bf16[2048,2048]{1,0:T(8,128)(2,1)} async-done(((bf16[256,2048]{1,0:T(8,128)(2,1)}), bf16[2048,2048]{1,0:T(8,128)(2,1)}) %all-gather.17.cloned.1.call-update) | async-done | bytes 8388624 | tf_op jit(solution)/shard_map/all_gather | solution.py:9
  209.0 5.2 reduce_sum.61
  214.2 24.9 %multiply_add_fusion = f32[4096,2048]{1,0:T(8,128)} fusion(f32[4096,2048]{1,0:T(8,128)} %param.12, bf16[256,2048]{1,0:T(8,128)(2,1)S(1)} %copy-done.4, bf16[256,2048]{1,0:T(8,128)(2,1)S(1)} %reduce_sum.61, bf16[256,2048]{1,0:T(8,128)(2,1)S(1)} %reduce_sum.60), kind=kOutput, calls=%fused_computation.1 | convolution fusion | flops 4315938816 | bytes 70254592 | tf_op jit(solution)/shard_map/dot_general | solution.py:57
  239.1 17.2 %select_convert_fusion.1 = (bf16[4096,512]{0,1:T(8,128)(2,1)S(1)}, f32[4096,512]{0,1:T(8,128)}) fusion(pred[4096]{0:T(1024)(128)(4,1)S(1)} %fusion.32, f32[2,512,512]{2,1,0:T(8,128)} %param.13, f32[4096,2048]{1,0:T(8,128)} %multiply_add_fusion), kind=kOutput, calls=%fused_computation.17 | convolution fusion | flops 12886999040 | bytes 22024192 | tf_op jit(solution)/shard_map/dot_general | solution.py:69
  256.4 1.9 copy-done.2
  258.3 0.8 slice_select_fusion
  259.6 45.4 %all-gather.19.cloned.1.call-done = bf16[2048,512]{0,1:T(8,128)(2,1)} async-done(((bf16[512,512]{0,1:T(8,128)(2,1)}), bf16[2048,512]{0,1:T(8,128)(2,1)}) %all-gather.19.cloned.1.call-update) | async-done | bytes 2097168 | tf_op jit(solution)/shard_map/all_gather | solution.py:9
  305.0 3.3 reshape.130
  308.3 2.8 reduce_sum.62
  311.1 9.4 fusion.7
  320.6 16.8 %fusion.11 = bf16[1,4096,512]{1,2,0:T(8,128)(2,1)S(1)} fusion(f32[4096,512]{1,0:T(8,128)S(1)} %fusion.7, f32[4096,2048]{1,0:T(8,128)} %multiply_add_fusion, pred[4096]{0:T(1024)(128)(4,1)S(1)} %fusion.30, f32[2,512,512]{2,1,0:T(8,128)S(1)} %copy-done.5), kind=kOutput, calls=%fused_computation.18 | convolution fusion | flops 12891193344 | bytes 22024192 | tf_op jit(solution)/shard_map/dot_general | solution.py:69
  337.4 4.6 maximum_select_fusion
  341.9 12.0 %copy.12 = bf16[1,4096,1024]{2,1,0:T(8,128)(2,1)} copy(bf16[1,4096,1024]{1,2,0:T(8,128)(2,1)} %maximum_select_fusion) | data formatting | bytes 16777216 | tf_op jit(solution)/shard_map/jit(_where)/select_n | solution.py:9
  354.0 301.6 %all-gather.13.cloned.1.call-done = bf16[8,4096,1024]{2,1,0:T(8,128)(2,1)} async-done(((bf16[1,4096,1024]{2,1,0:T(8,128)(2,1)}), bf16[8,4096,1024]{2,1,0:T(8,128)(2,1)}) %all-gather.13.cloned.1.call-update) | async-done | bytes 67108880 | tf_op jit(solution)/shard_map/all_gather | solution.py:9
  655.6 26.2 %reduce_sum.63 = bf16[4096,1024]{1,0:T(8,128)(2,1)} reduce(bf16[8,4096,1024]{2,1,0:T(8,128)(2,1)} %all-gather.13.cloned.1.call-done, bf16[]{:T(256)} %constant.68.clone.1), dimensions={0}, to_apply=%region_6.7 | reduce | flops 29360128 | bytes 75497472 | tf_op jit(solution)/shard_map/reduce_sum | solution.py:9
  681.8 11.3 convert_element_type.53
  693.0 6.7 fusion.12
  699.8 13.5 %broadcast_in_dim.81 = f32[4096,2048]{1,0:T(8,128)} broadcast(f32[]{:T(128)} %constant.64.clone.1), dimensions={} | broadcast | bytes 33554436 | tf_op jit(solution)/shard_map/jit(_where)/broadcast_in_dim | solution.py:96
  713.2 78.1 %dynamic_update_slice.3 = f32[4096,2048]{1,0:T(8,128)} dynamic-update-slice(f32[4096,2048]{1,0:T(8,128)} %broadcast_in_dim.81, f32[4096,1024]{1,0:T(8,128)} %convert_element_type.53, s32[]{:T(128)} %constant.32.clone.1, s32[]{:T(128)S(6)} %min.4) | dynamic-update-slice | bytes 33554436 | tf_op jit(solution)/shard_map/dynamic_update_slice | solution.py:92
  791.3 195.3 %all-gather.21.cloned.1.call-done = bf16[8192,1024]{1,0:T(8,128)(2,1)} async-done(((bf16[2048,1024]{1,0:T(8,128)(2,1)}), bf16[8192,1024]{1,0:T(8,128)(2,1)}) %all-gather.21.cloned.1.call-update) | async-done | bytes 16777232 | tf_op jit(solution)/shard_map/all_gather | solution.py:9
  986.6 12.0 %reduce_sum.64 = bf16[2048,1024]{1,0:T(8,128)(2,1)} reduce(bf16[4,2048,1024]{2,1,0:T(8,128)(2,1)} %bitcast.34, bf16[]{:T(256)} %constant.68.clone.1), dimensions={0}, to_apply=%region_7.8 | reduce | flops 6291456 | bytes 20971522 | tf_op jit(solution)/shard_map/reduce_sum | solution.py:9
  998.7 5.2 fusion.58
  1003.9 123.6 %select_select_fusion = f32[4096,2048]{1,0:T(8,128)} fusion(f32[4096,2048]{1,0:T(8,128)} %dynamic_update_slice.3, f32[4096,2048]{1,0:T(8,128)} %multiply_add_fusion, pred[2048]{0:T(1024)(128)(4,1)S(1)} %get-tuple-element.14, pred[2048]{0:T(1024)(128)(4,1)S(1)} %get-tuple-element.13, pred[4096]{0:T(1024)(128)(4,1)S(1)} %get-tuple-element.12, ...), kind=kOutput, calls=%fused_computation | convolution fusion | flops 103121158144 | bytes 117452800 | tf_op jit(solution)/shard_map/dot_general | solution.py:90
  (34 shorter events, 4.3 us)
Async XLA Ops:
  6.5 1.6 copy-start
  6.5 89.7 %all-gather.11.cloned.1.call-start = ((), (), s32[]{:S(2)}) async-start(), calls=%async_computation | async-start | bytes 1310720 | tf_op jit(solution)/shard_map/all_gather | solution.py:51
  68.5 84.3 %all-gather.15.cloned.1.call-start = ((), (), s32[]{:S(2)}) async-start(), calls=%async_computation.2 | async-start | bytes 9437184 | tf_op jit(solution)/shard_map/all_gather | solution.py:9
  99.0 110.0 %all-gather.17.cloned.1.call-start = ((), (), s32[]{:S(2)}) async-start(), calls=%async_computation.3 | async-start | bytes 9437184 | tf_op jit(solution)/shard_map/all_gather | solution.py:9
  99.8 205.2 %all-gather.19.cloned.1.call-start = ((), (), s32[]{:S(2)}) async-start(), calls=%async_computation.4 | async-start | bytes 2621440 | tf_op jit(solution)/shard_map/all_gather | solution.py:9
  152.8 61.4 %copy-start.4 = (bf16[256,2048]{1,0:T(8,128)(2,1)S(1)}, bf16[256,2048]{1,0:T(8,128)(2,1)}, u32[]{:S(2)}) copy-start(bf16[256,2048]{1,0:T(8,128)(2,1)} %all-gather.11.cloned.1.call-done) | copy-start | bytes 3145732
  256.4 1.9 copy-start.2
  259.2 396.4 %all-gather.13.cloned.1.call-start = ((), (), s32[]{:S(2)}) async-start(), calls=%async_computation.1 | async-start | bytes 75497472 | tf_op jit(solution)/shard_map/all_gather | solution.py:9
  311.1 9.4 copy-start.5
  320.6 16.8 %copy-start.3 = (bf16[4096,512]{0,1:T(8,128)(2,1)S(1)}, bf16[4096,512]{0,1:T(8,128)(2,1)}, u32[]{:S(2)}) copy-start(bf16[4096,512]{0,1:T(8,128)(2,1)} %copy-done.2) | copy-start | bytes 12582916
  353.9 632.7 %all-gather.21.cloned.1.call-start = ((), (), s32[]{:S(2)}) async-start(), calls=%async_computation.5 | async-start | bytes 20971520 | tf_op jit(solution)/shard_map/all_gather | solution.py:9
  1003.9 123.6 %copy-start.1 = (bf16[1024,1024]{1,0:T(8,128)(2,1)S(1)}, bf16[1024,1024]{1,0:T(8,128)(2,1)}, u32[]{:S(2)}) copy-start(bf16[1024,1024]{1,0:T(8,128)(2,1)} %param.8) | copy-start | bytes 6291460
Sparse Core Ops, SparseCore 0:
  68.7 27.5 all-gather.10
  99.1 53.6 all-gather.14
  154.7 54.2 all-gather.16
  259.3 45.6 all-gather.18
  354.0 301.5 all-gather.12
  699.8 286.7 all-gather.20
